TPU v7x, 32 devices: a whole 2x2x4 slice. The times are simulated.
32 devices in a mesh: dp: 8 (over z, x), seq: 4 (over y, core).
Axes of the slice: x: 2, y: 2, z: 4, core: 2. Of those that a mesh axis runs over, the one named last changes fastest.
Arguments:
- field: bfloat16 [8, 2048, 1024], P('dp', 'seq'), may hold values from -6 to 6
- eq_embed: bfloat16 [8, 512, 1024], P('dp', 'seq'), may hold values from -6 to 6
- eq_len: int32 [8], replicated, may hold values from 1 to 512, 2048 in all
- owner: int32 [8], replicated, may hold values from 0 to 7, as said below
- norm_gain: float32 [1024], replicated, may hold values from 0.1 to 1.9
- w_qkv: bfloat16 [1024, 3072], replicated, may hold values from -0.176776695 to 0.176776695
- w_out: bfloat16 [1024, 1024], replicated, may hold values from -0.1875 to 0.1875
- cross_gain: float32 [1024], replicated, may hold values from 0.1 to 1.9
- w_cq: bfloat16 [1024, 1024], replicated, may hold values from -0.125 to 0.125
- w_ckv: bfloat16 [1024, 2048], replicated, may hold values from -0.125 to 0.125
- w_cout: bfloat16 [1024, 1024], replicated, may hold values from -0.1875 to 0.1875
Outputs:
- joined: bfloat16 [8, 2048, 1024], P('dp', 'seq')
Inputs may be any that keep to these rules, and one draw needn't show every extreme that they name: `owner`: every slot number appears exactly once. `eq_len`: some slot has all 512 tokens real.
All inputs are finite; a program needn't handle non-finite values.
Results may differ from a plain program's by a relative error of at most 0.0055.
Values may be sent and summed in bfloat16 or wider, within the bound.
A program may use at most 128 MiB of HBM per device.

v0:
```python
import jax
import jax.numpy as jnp
from jax import lax
from jax.sharding import PartitionSpec as P

D = 1024
HEADS = 16
HEAD_DIM = 64


def normalize(values, gain):
    return values * lax.rsqrt(jnp.mean(values * values, axis=-1, keepdims=True) + 1e-06) * gain


def attend(query, keys, values, valid):
    rows = query.shape[0]
    heads = query.shape[1]
    depth = query.shape[2]
    block = min(512, rows)
    scale = depth ** (-0.5)

    def one_block(query_block):
        scores = (
            jnp.einsum("qhd,khd->hqk", query_block, keys, preferred_element_type=jnp.float32)
            * scale
        )
        expo = jnp.where(valid[None, None, :], jnp.exp(scores), 0.0)
        weights = (expo / jnp.sum(expo, axis=-1, keepdims=True)).astype(jnp.bfloat16)
        return jnp.einsum(
            "hqk,khd->qhd", weights, values, preferred_element_type=jnp.float32
        ).astype(jnp.bfloat16)

    blocks = lax.map(one_block, query.reshape(rows // block, block, heads, depth))
    return blocks.reshape(rows, heads * depth)


def pick_slot(wanted, carry, piece):
    inside = (wanted >= 0) & (wanted < piece.shape[0])
    picked = lax.dynamic_index_in_dim(
        piece, jnp.clip(wanted, 0, piece.shape[0] - 1), 0, keepdims=False
    )
    return jnp.where(inside, picked, carry)


def per_device(
    field, eq_embed, eq_len, owner, norm_gain, w_qkv, w_out, cross_gain, w_cq, w_ckv, w_cout
):
    tokens = field[0].astype(jnp.float32)
    tok_rows = tokens.shape[0]
    groups = lax.axis_size("seq")
    head_count = HEADS // groups
    normed = normalize(tokens, norm_gain).astype(jnp.bfloat16)
    projected = jnp.dot(normed, w_qkv, preferred_element_type=jnp.float32).astype(jnp.bfloat16)
    stacked = projected.reshape(tok_rows, 3, D)
    local_heads = lax.all_to_all(stacked, "seq", split_axis=2, concat_axis=0, tiled=True)
    seq_rows = local_heads.shape[0]
    split = local_heads.reshape(seq_rows, 3, head_count, HEAD_DIM)
    every = jnp.ones((seq_rows,), dtype=bool)
    attended = attend(split[:, 0], split[:, 1], split[:, 2], every)
    merged = lax.all_to_all(attended, "seq", split_axis=0, concat_axis=1, tiled=True)
    mixed = tokens + jnp.dot(merged, w_out, preferred_element_type=jnp.float32)
    cross_in = normalize(mixed, cross_gain).astype(jnp.bfloat16)
    cross_q = jnp.dot(cross_in, w_cq, preferred_element_type=jnp.float32).astype(jnp.bfloat16)
    slot = lax.dynamic_index_in_dim(owner, lax.axis_index("dp"), 0, keepdims=False)
    length = lax.dynamic_index_in_dim(eq_len, slot, 0, keepdims=False)
    eq_rows = eq_embed.shape[1]
    empty = jnp.zeros(eq_embed.shape[1:], jnp.bfloat16)
    owned_rows = pick_slot(slot, empty, lax.all_gather(eq_embed, "dp", axis=0, tiled=True))
    owned_kv = jnp.dot(owned_rows, w_ckv, preferred_element_type=jnp.float32).astype(jnp.bfloat16)
    whole_kv = lax.all_gather(owned_kv, "seq", axis=0, tiled=True)
    whole_kv = whole_kv.reshape(eq_rows * groups, 2, HEADS, HEAD_DIM)
    valid = jnp.arange(eq_rows * groups, dtype=jnp.int32) < length
    cross_att = attend(
        cross_q.reshape(tok_rows, HEADS, HEAD_DIM), whole_kv[:, 0], whole_kv[:, 1], valid
    )
    joined = mixed + jnp.dot(cross_att, w_cout, preferred_element_type=jnp.float32)
    return joined.astype(jnp.bfloat16)[None]


def solution(mesh):
    in_specs = (
        P("dp", "seq", None),
        P("dp", "seq", None),
        P(),
        P(),
        P(),
        P(),
        P(),
        P(),
        P(),
        P(),
        P(),
    )
    out_specs = P("dp", "seq", None)
    return jax.shard_map(
        per_device, mesh=mesh, in_specs=in_specs, out_specs=out_specs, check_vma=False
    )
```

profile of v0, /device:TPU:0, one launch (start us, length us, event | category | flops | bytes accessed | tf_op | source)
XLA Modules:
  0.0 189.4 jit_solution(14081409868850262506)
XLA Ops:
  8.8 8.3 %convolution_convert_fusion = bf16[512,3072]{1,0:T(8,128)(2,1)} fusion(bf16[1024,3072]{1,0:T(8,128)(2,1)} %param.18, bf16[1,512,1024]{2,1,0:T(8,128)(2,1)} %param.13, f32[1024]{0:T(1024)} %param.17, f32[512]{0:T(512)S(1)} %add_rsqrt_fusion.1), kind=kOutput, calls=%fused_computation.16 | convolution fusion | flops 3224895488 | bytes 10491904 | tf_op jit(solution)/shard_map/dot_general | solution.py:53
  17.1 4.7 %copy.28 = bf16[512,3072]{0,1:T(8,128)(2,1)} copy(bf16[512,3072]{1,0:T(8,128)(2,1)} %convolution_convert_fusion) | data formatting | bytes 6291456 | tf_op jit(solution)/shard_map/convert_element_type | solution.py:53
  21.7 6.5 %copy.29 = bf16[512,3,1024]{0,1,2:T(4,128)(2,1)} copy(bf16[512,3,1024]{0,2,1:T(8,128)(2,1)} %bitcast.75) | data formatting | bytes 6291456 | tf_op jit(solution)/shard_map/reshape | solution.py:54
  28.3 5.0 %all-to-all-start = ((bf16[512,3,1024]{0,1,2:T(4,128)(2,1)}), bf16[512,3,1024]{0,1,2:T(4,128)(2,1)}, u32[]{:S(2)}, u32[]{:S(2)}) async-start(bf16[512,3,1024]{0,1,2:T(4,128)(2,1)} %copy.29), calls=%async_computation | async-start | bytes 8388608 | tf_op jit(solution)/shard_map/all_to_all | solution.py:55
  35.8 46.4 %all-to-all-done = bf16[512,3,1024]{0,1,2:T(4,128)(2,1)} async-done(((bf16[512,3,1024]{0,1,2:T(4,128)(2,1)}), bf16[512,3,1024]{0,1,2:T(4,128)(2,1)}, u32[]{:S(2)}, u32[]{:S(2)}) %all-to-all-start) | async-done | bytes 3145760 | tf_op jit(solution)/shard_map/all_to_all | solution.py:55
  82.2 3.0 %copy.30 = bf16[512,3,1024]{0,2,1:T(8,128)(2,1)S(1)} copy(bf16[512,3,1024]{0,1,2:T(4,128)(2,1)} %all-to-all-done) | data formatting | bytes 6291456 | tf_op jit(solution)/shard_map/all_to_all | solution.py:55
  85.1 4.1 %copy.31 = bf16[4,512,3,256]{1,0,3,2:T(4,128)(2,1)} copy(bf16[4,512,3,256]{1,3,0,2:T(8,128)(2,1)S(1)} %bitcast.76) | data formatting | bytes 6291456 | tf_op jit(solution)/shard_map/all_to_all | solution.py:55
  89.2 6.1 %reshape.50 = bf16[2048,3,4,64]{0,3,2,1:T(8,128)(2,1)} reshape(bf16[4,512,3,256]{1,0,3,2:T(4,128)(2,1)} %copy.31) | data formatting | bytes 6291456 | tf_op jit(solution)/shard_map/reshape | solution.py:57
  95.3 3.6 %slice_bitcast_fusion.4 = (bf16[2048,4,64]{0,2,1:T(8,128)(2,1)}, bf16[2048,4,64]{0,2,1:T(8,128)(2,1)S(1)}, bf16[2048,1,4,64]{0,3,2,1:T(8,128)(2,1)}) fusion(bf16[2048,3,4,64]{0,3,2,1:T(8,128)(2,1)} %reshape.50), kind=kLoop, calls=%fused_computation.33 | loop fusion | bytes 6291456 | tf_op jit(solution)/shard_map/squeeze | solution.py:59
  103.9 3.8 %convolution_convert_fusion.1 = bf16[128,2048]{1,0:T(8,128)(2,1)} fusion(bf16[1024,2048]{1,0:T(8,128)(2,1)} %param.22, bf16[8,128,1024]{2,1,0:T(8,128)(2,1)} %all-gather.3.cloned.1.call-done, s32[]{:T(128)S(6)} %min.4, pred[]{:T(512)S(6)} %and.4), kind=kOutput, calls=%fused_computation.20 | convolution fusion | flops 537264128 | bytes 4980741 | tf_op jit(solution)/shard_map/dot_general | solution.py:69
  107.8 33.5 %while.2 = (s32[]{:T(128)}, bf16[4,512,4,64]{1,3,2,0:T(8,128)(2,1)}, bf16[4,512,4,64]{1,3,2,0:T(8,128)(2,1)}, bf16[2048,4,64]{0,2,1:T(8,128)(2,1)S(1)}, bf16[2048,4,64]{0,2,1:T(8,128)(2,1)}, /*index=5*/s32[]{:T(128)}) while((s32[]{:T(128)}, bf16[4,512,4,64]{1,3,2,0:T(8,128)(2,1)}, bf16[4,512,4,64]{1,3,2,0:T(8,128)(2,1)}, ...), condition=%wide.region_3.4_spmd, body=%wide.region_1.3_spmd.sunk | while | flops 1094842368 | bytes 40386672 | solution.py:33
  107.8 4.0 %fusion.49 = (f32[4,512]{1,0:T(4,128)S(1)}, f32[4,512,2048]{2,1,0:T(8,128)S(1)}) fusion(bf16[2048,4,64]{0,2,1:T(8,128)(2,1)S(1)} %get-tuple-element.135, bf16[4,512,4,64]{1,3,2,0:T(8,128)(2,1)} %get-tuple-element.134, s32[]{:T(128)S(6)} %copy.40), kind=kOutput, calls=%fused_computation.2.clone.1 | convolution fusion | flops 545257472 | bytes 18096132 | tf_op jit(solution)/shard_map/while/body/eval_jaxpr/qhd,khd->hqk/dot_general | solution.py:24
  111.9 4.3 %fusion.50 = bf16[4,512,4,64]{1,3,2,0:T(8,128)(2,1)} fusion(bf16[4,512,4,64]{1,3,2,0:T(8,128)(2,1)} %get-tuple-element.127, s32[]{:T(128)S(6)} %copy.40, bf16[2048,4,64]{0,2,1:T(8,128)(2,1)S(1)} %copy-done.4, f32[4,512,2048]{2,1,0:T(8,128)S(1)} %get-tuple-element.118, f32[4,512]{1,0:T(4,128)S(1)} %get-tuple-element.119), kind=kOutput, calls=%fused_computation.6.clone.1 | convolution fusion | flops 549584896 | bytes 18096132 | tf_op jit(solution)/shard_map/while/body/eval_jaxpr/hqk,khd->qhd/dot_general | solution.py:29
  116.2 4.1 %fusion.49 = (f32[4,512]{1,0:T(4,128)S(1)}, f32[4,512,2048]{2,1,0:T(8,128)S(1)}) fusion(bf16[2048,4,64]{0,2,1:T(8,128)(2,1)S(1)} %get-tuple-element.135, bf16[4,512,4,64]{1,3,2,0:T(8,128)(2,1)} %get-tuple-element.134, s32[]{:T(128)S(6)} %copy.40), kind=kOutput, calls=%fused_computation.2.clone.1 | convolution fusion | flops 545257472 | bytes 18096132 | tf_op jit(solution)/shard_map/while/body/eval_jaxpr/qhd,khd->hqk/dot_general | solution.py:24
  120.3 4.3 %fusion.50 = bf16[4,512,4,64]{1,3,2,0:T(8,128)(2,1)} fusion(bf16[4,512,4,64]{1,3,2,0:T(8,128)(2,1)} %get-tuple-element.127, s32[]{:T(128)S(6)} %copy.40, bf16[2048,4,64]{0,2,1:T(8,128)(2,1)S(1)} %copy-done.4, f32[4,512,2048]{2,1,0:T(8,128)S(1)} %get-tuple-element.118, f32[4,512]{1,0:T(4,128)S(1)} %get-tuple-element.119), kind=kOutput, calls=%fused_computation.6.clone.1 | convolution fusion | flops 549584896 | bytes 18096132 | tf_op jit(solution)/shard_map/while/body/eval_jaxpr/hqk,khd->qhd/dot_general | solution.py:29
  124.6 4.0 %fusion.49 = (f32[4,512]{1,0:T(4,128)S(1)}, f32[4,512,2048]{2,1,0:T(8,128)S(1)}) fusion(bf16[2048,4,64]{0,2,1:T(8,128)(2,1)S(1)} %get-tuple-element.135, bf16[4,512,4,64]{1,3,2,0:T(8,128)(2,1)} %get-tuple-element.134, s32[]{:T(128)S(6)} %copy.40), kind=kOutput, calls=%fused_computation.2.clone.1 | convolution fusion | flops 545257472 | bytes 18096132 | tf_op jit(solution)/shard_map/while/body/eval_jaxpr/qhd,khd->hqk/dot_general | solution.py:24
  128.6 4.3 %fusion.50 = bf16[4,512,4,64]{1,3,2,0:T(8,128)(2,1)} fusion(bf16[4,512,4,64]{1,3,2,0:T(8,128)(2,1)} %get-tuple-element.127, s32[]{:T(128)S(6)} %copy.40, bf16[2048,4,64]{0,2,1:T(8,128)(2,1)S(1)} %copy-done.4, f32[4,512,2048]{2,1,0:T(8,128)S(1)} %get-tuple-element.118, f32[4,512]{1,0:T(4,128)S(1)} %get-tuple-element.119), kind=kOutput, calls=%fused_computation.6.clone.1 | convolution fusion | flops 549584896 | bytes 18096132 | tf_op jit(solution)/shard_map/while/body/eval_jaxpr/hqk,khd->qhd/dot_general | solution.py:29
  132.9 4.0 %fusion.49 = (f32[4,512]{1,0:T(4,128)S(1)}, f32[4,512,2048]{2,1,0:T(8,128)S(1)}) fusion(bf16[2048,4,64]{0,2,1:T(8,128)(2,1)S(1)} %get-tuple-element.135, bf16[4,512,4,64]{1,3,2,0:T(8,128)(2,1)} %get-tuple-element.134, s32[]{:T(128)S(6)} %copy.40), kind=kOutput, calls=%fused_computation.2.clone.1 | convolution fusion | flops 545257472 | bytes 18096132 | tf_op jit(solution)/shard_map/while/body/eval_jaxpr/qhd,khd->hqk/dot_general | solution.py:24
  137.0 4.3 %fusion.50 = bf16[4,512,4,64]{1,3,2,0:T(8,128)(2,1)} fusion(bf16[4,512,4,64]{1,3,2,0:T(8,128)(2,1)} %get-tuple-element.127, s32[]{:T(128)S(6)} %copy.40, bf16[2048,4,64]{0,2,1:T(8,128)(2,1)S(1)} %copy-done.4, f32[4,512,2048]{2,1,0:T(8,128)S(1)} %get-tuple-element.118, f32[4,512]{1,0:T(4,128)S(1)} %get-tuple-element.119), kind=kOutput, calls=%fused_computation.6.clone.1 | convolution fusion | flops 549584896 | bytes 18096132 | tf_op jit(solution)/shard_map/while/body/eval_jaxpr/hqk,khd->qhd/dot_general | solution.py:29
  141.3 3.7 %all-to-all-start.1 = ((bf16[4,512,256]{1,2,0:T(8,128)(2,1)}), bf16[4,512,256]{1,2,0:T(8,128)(2,1)S(1)}, u32[]{:S(2)}, u32[]{:S(2)}) async-start(bf16[4,512,256]{1,2,0:T(8,128)(2,1)} %bitcast.80), calls=%async_computation.1 | async-start | bytes 2097152 | tf_op jit(solution)/shard_map/all_to_all | solution.py:60
  148.0 11.3 %all-to-all-done.1 = bf16[4,512,256]{1,2,0:T(8,128)(2,1)S(1)} async-done(((bf16[4,512,256]{1,2,0:T(8,128)(2,1)}), bf16[4,512,256]{1,2,0:T(8,128)(2,1)S(1)}, u32[]{:S(2)}, u32[]{:S(2)}) %all-to-all-start.1) | async-done | bytes 1048608 | tf_op jit(solution)/shard_map/all_to_all | solution.py:60
  167.1 3.9 %copy.33 = bf16[512,2048]{0,1:T(8,128)(2,1)} copy(bf16[512,2048]{1,0:T(8,128)(2,1)} %all-gather.5.cloned.1.call-done) | data formatting | bytes 4194304 | tf_op jit(solution)/shard_map/all_gather | solution.py:70
  171.0 5.5 %fusion.10 = (f32[16,512]{1,0:T(8,128)S(1)}, f32[16,512,512]{1,2,0:T(8,128)S(1)}) fusion(pred[512]{0:T(512)(128)(4,1)S(1)} %iota_compare_fusion, bf16[512,16,64]{0,2,1:T(8,128)(2,1)S(1)} %bitcast.81, bf16[512,2,16,64]{0,3,2,1:T(8,128)(2,1)} %bitcast.78), kind=kOutput, calls=%fused_computation.14 | convolution fusion | flops 549445632 | bytes 18907648 | tf_op jit(solution)/shard_map/while/body/eval_jaxpr/qhd,khd->hqk/dot_general | solution.py:24
  176.6 3.7 %fusion.15 = bf16[16,64,512]{2,1,0:T(8,128)(2,1)S(1)} fusion(f32[16,512,512]{1,2,0:T(8,128)S(1)} %get-tuple-element.84, f32[16,512]{1,0:T(8,128)S(1)} %get-tuple-element.83, pred[512]{0:T(512)(128)(4,1)S(1)} %iota_compare_fusion, bf16[512,2,16,64]{0,3,2,1:T(8,128)(2,1)S(1)} %bitcast.79), kind=kOutput, calls=%fused_computation.27 | convolution fusion | flops 554172416 | bytes 18907648 | tf_op jit(solution)/shard_map/while/body/eval_jaxpr/hqk,khd->qhd/dot_general | solution.py:29
  (45 shorter events, 19.5 us)
Async XLA Ops:
  6.5 152.7 %copy-start = (bf16[1024,1024]{1,0:T(8,128)(2,1)S(1)}, bf16[1024,1024]{1,0:T(8,128)(2,1)}, u32[]{:S(2)}) copy-start(bf16[1024,1024]{1,0:T(8,128)(2,1)} %param.19) | copy-start | bytes 6291460
  6.5 97.4 %all-gather.3.cloned.1.call-start = ((), (), s32[]{:S(2)}) async-start(), calls=%async_computation.2 | async-start | bytes 2359296 | tf_op jit(solution)/shard_map/all_gather | solution.py:68
  28.3 5.2 %copy-start.8 = (s32[8]{0:T(128)S(1)}, s32[8]{0:T(128)}, u32[]{:S(2)}) copy-start(s32[8]{0:T(128)} %param.16) | copy-start | bytes 100
  28.3 53.9 %all-to-all-start = ((bf16[512,3,1024]{0,1,2:T(4,128)(2,1)}), bf16[512,3,1024]{0,1,2:T(4,128)(2,1)}, u32[]{:S(2)}, u32[]{:S(2)}) async-start(bf16[512,3,1024]{0,1,2:T(4,128)(2,1)} %copy.29), calls=%async_computation | async-start | bytes 8388608 | tf_op jit(solution)/shard_map/all_to_all | solution.py:55
  33.3 133.8 %all-gather.5.cloned.1.call-start = ((), (), s32[]{:S(2)}) async-start(), calls=%async_computation.3 | async-start | bytes 2621440 | tf_op jit(solution)/shard_map/all_gather | solution.py:70
  107.8 38.9 %copy-start.9 = (s32[8]{0:T(128)S(1)}, s32[8]{0:T(128)}, u32[]{:S(2)}) copy-start(s32[8]{0:T(128)} %param.15) | copy-start | bytes 100
  107.8 4.1 %copy-start.4 = (bf16[2048,4,64]{0,2,1:T(8,128)(2,1)S(1)}, bf16[2048,4,64]{0,2,1:T(8,128)(2,1)}, u32[]{:S(2)}) copy-start(bf16[2048,4,64]{0,2,1:T(8,128)(2,1)} %get-tuple-element.136) | copy-start | bytes 3145732 | tf_op jit(solution)/shard_map/while
  116.2 4.1 %copy-start.4 = (bf16[2048,4,64]{0,2,1:T(8,128)(2,1)S(1)}, bf16[2048,4,64]{0,2,1:T(8,128)(2,1)}, u32[]{:S(2)}) copy-start(bf16[2048,4,64]{0,2,1:T(8,128)(2,1)} %get-tuple-element.136) | copy-start | bytes 3145732 | tf_op jit(solution)/shard_map/while
  124.6 4.0 %copy-start.4 = (bf16[2048,4,64]{0,2,1:T(8,128)(2,1)S(1)}, bf16[2048,4,64]{0,2,1:T(8,128)(2,1)}, u32[]{:S(2)}) copy-start(bf16[2048,4,64]{0,2,1:T(8,128)(2,1)} %get-tuple-element.136) | copy-start | bytes 3145732 | tf_op jit(solution)/shard_map/while
  132.9 4.0 %copy-start.4 = (bf16[2048,4,64]{0,2,1:T(8,128)(2,1)S(1)}, bf16[2048,4,64]{0,2,1:T(8,128)(2,1)}, u32[]{:S(2)}) copy-start(bf16[2048,4,64]{0,2,1:T(8,128)(2,1)} %get-tuple-element.136) | copy-start | bytes 3145732 | tf_op jit(solution)/shard_map/while
  141.3 18.0 %all-to-all-start.1 = ((bf16[4,512,256]{1,2,0:T(8,128)(2,1)}), bf16[4,512,256]{1,2,0:T(8,128)(2,1)S(1)}, u32[]{:S(2)}, u32[]{:S(2)}) async-start(bf16[4,512,256]{1,2,0:T(8,128)(2,1)} %bitcast.80), calls=%async_computation.1 | async-start | bytes 2097152 | tf_op jit(solution)/shard_map/all_to_all | solution.py:60
  159.2 4.1 %copy-start.5 = (bf16[1024,1024]{1,0:T(8,128)(2,1)S(1)}, bf16[1024,1024]{1,0:T(8,128)(2,1)}, u32[]{:S(2)}) copy-start(bf16[1024,1024]{1,0:T(8,128)(2,1)} %param.21) | copy-start | bytes 6291460
  159.2 4.1 %copy-start.7 = (f32[1024]{0:T(1024)S(1)}, f32[1024]{0:T(1024)}, u32[]{:S(2)}) copy-start(f32[1024]{0:T(1024)} %param.20) | copy-start | bytes 12292
  162.0 1.3 copy-start.1
  171.0 5.5 %copy-start.3 = (bf16[512,2048]{0,1:T(8,128)(2,1)S(1)}, bf16[512,2048]{0,1:T(8,128)(2,1)}, u32[]{:S(2)}) copy-start(bf16[512,2048]{0,1:T(8,128)(2,1)} %copy.33) | copy-start | bytes 6291460
  176.6 3.8 %copy-start.2 = (f32[512,1024]{1,0:T(8,128)S(1)}, f32[512,1024]{1,0:T(8,128)}, u32[]{:S(2)}) copy-start(f32[512,1024]{1,0:T(8,128)} %copy-done.1) | copy-start | bytes 6291460
  176.6 3.8 %copy-start.6 = (bf16[1024,1024]{1,0:T(8,128)(2,1)S(1)}, bf16[1024,1024]{1,0:T(8,128)(2,1)}, u32[]{:S(2)}) copy-start(bf16[1024,1024]{1,0:T(8,128)(2,1)} %param.23) | copy-start | bytes 6291460
Sparse Core Ops, SparseCore 0:
  9.5 51.9 all-gather.2
  107.9 23.6 all-gather.4
where the time goes:
time: 190 us; the launch traced here: 189 us
  matrix products  62 us (33%)
  waiting for transfers between devices  58.4 us (31%)
  local copies, waits for them, and re-layouts  41 us (22%)
  between operations  16.9 us (9%)
  starting transfers between devices  8.93 us (5%)
  other arithmetic  2.16 us (1%)
    all_to_all x1, waiting for transfers between devices, per_device(): lax.all_to_all(stacked, 'seq', split_axis=2, concat_axis=0, tiled=True)  46.4 us
    dot_general x5, matrix products, one_block(): jnp.einsum('qhd,khd->hqk', query_block, keys, preferred_element_type=jnp....  21.7 us
    dot_general x5, matrix products, one_block(): jnp.einsum('hqk,khd->qhd', weights, values, preferred_element_type=jnp.fl...  20.9 us
    all_to_all x1, waiting for transfers between devices, per_device(): lax.all_to_all(attended, 'seq', split_axis=0, concat_axis=1, tiled=True)  11.3 us
    dot_general x1, matrix products, per_device(): jnp.dot(normed, w_qkv, preferred_element_type=jnp.float32)  8.28 us
    all_to_all x2, local copies, waits for them, and re-layouts, per_device(): lax.all_to_all(stacked, 'seq', split_axis=2, concat_axis=0, tiled=True)  7.07 us
    reshape x1, local copies, waits for them, and re-layouts, per_device(): stacked = projected.reshape(tok_rows, 3, D)  6.53 us
    reshape x1, local copies, waits for them, and re-layouts, per_device(): split = local_heads.reshape(seq_rows, 3, head_count, HEAD_DIM)  6.1 us
  transfers between devices with their start and end apart: 4, of which 2 were waited for; matrix products, arithmetic and copies ran while one was open for 45% of the time, Pallas kernels for 0%

commit v1 on v0

--- a/solution.py
+++ b/solution.py
@@ -52,7 +52,10 @@
     normed = normalize(tokens, norm_gain).astype(jnp.bfloat16)
     projected = jnp.dot(normed, w_qkv, preferred_element_type=jnp.float32).astype(jnp.bfloat16)
     stacked = projected.reshape(tok_rows, 3, D)
-    local_heads = lax.all_to_all(stacked, "seq", split_axis=2, concat_axis=0, tiled=True)
+    local_heads = jnp.concatenate(
+        lax.all_to_all(jnp.stack(jnp.split(stacked, lax.axis_size("seq"), axis=2)), "seq", 0, 0),
+        axis=0,
+    )
     seq_rows = local_heads.shape[0]
     split = local_heads.reshape(seq_rows, 3, head_count, HEAD_DIM)
     every = jnp.ones((seq_rows,), dtype=bool)

time: 190 us -> 175 us (0.921)
  waiting for transfers between devices: 58.4 us -> 47.4 us
  local copies, waits for them, and re-layouts: 41 us -> 35.5 us
    reshape x2 -> x0, local copies, waits for them, and re-layouts: 12.6 us -> none  [the longest x1 6.53 us: per_device(): stacked = projected.reshape(tok_rows, 3, D)]
    all_to_all x1, waiting for transfers between devices: 46.4 us -> 35.3 us  [per_device(): lax.all_to_all(jnp.stack(jnp.split(stacked, lax.axis_size('seq'), axis=2)...]
    another operation x0 -> x2, local copies, waits for them, and re-layouts: none -> 8.15 us  [the longest x1 6.1 us: per_device(): split = local_heads.reshape(seq_rows, 3, head_count, HEAD_DIM)]
    another operation x0 -> x1, other arithmetic: none -> 1.9 us  [per_device(): jnp.stack(jnp.split(stacked, lax.axis_size('seq'), axis=2))]
    all_to_all x2 -> x1, local copies, waits for them, and re-layouts: 7.07 us -> 5.98 us  [per_device(): lax.all_to_all(jnp.stack(jnp.split(stacked, lax.axis_size('seq'), axis=2)...]
  transfers between devices with their start and end apart: 4 -> 4, of which waited for: 2 -> 2; matrix products, arithmetic and copies ran while one was open for 45% -> 46% of each run, Pallas kernels for 0% -> 0%
where the time goes in v1:
time: 175 us; the launch traced here: 174 us
  matrix products  62 us (35%)
  waiting for transfers between devices  47.4 us (27%)
  local copies, waits for them, and re-layouts  35.5 us (20%)
  between operations  16.9 us (10%)
  starting transfers between devices  8.54 us (5%)
  other arithmetic  4.03 us (2%)
    all_to_all x1, waiting for transfers between devices, per_device(): lax.all_to_all(jnp.stack(jnp.split(stacked, lax.axis_size('seq'), axis=2)...  35.3 us
    dot_general x5, matrix products, one_block(): jnp.einsum('qhd,khd->hqk', query_block, keys, preferred_element_type=jnp....  21.7 us
    dot_general x5, matrix products, one_block(): jnp.einsum('hqk,khd->qhd', weights, values, preferred_element_type=jnp.fl...  20.9 us
    all_to_all x1, waiting for transfers between devices, per_device(): lax.all_to_all(attended, 'seq', split_axis=0, concat_axis=1, tiled=True)  11.3 us
    dot_general x1, matrix products, per_device(): jnp.dot(normed, w_qkv, preferred_element_type=jnp.float32)  8.28 us
    another operation x1, local copies, waits for them, and re-layouts, per_device(): split = local_heads.reshape(seq_rows, 3, head_count, HEAD_DIM)  6.1 us
    all_to_all x1, local copies, waits for them, and re-layouts, per_device(): lax.all_to_all(jnp.stack(jnp.split(stacked, lax.axis_size('seq'), axis=2)...  5.98 us
    all_to_all x1, starting transfers between devices, per_device(): lax.all_to_all(jnp.stack(jnp.split(stacked, lax.axis_size('seq'), axis=2)...  4.8 us
  transfers between devices with their start and end apart: 4, of which 2 were waited for; matrix products, arithmetic and copies ran while one was open for 46% of the time, Pallas kernels for 0%

profile of v1, /device:TPU:0, one launch (start us, length us, event | category | flops | bytes accessed | tf_op | source)
XLA Modules:
  0.0 174.4 jit_solution(8106904559421201490)
XLA Ops:
  8.8 8.3 %convolution_convert_fusion = bf16[512,3072]{1,0:T(8,128)(2,1)} fusion(bf16[1024,3072]{1,0:T(8,128)(2,1)} %param.18, bf16[1,512,1024]{2,1,0:T(8,128)(2,1)} %param.13, f32[1024]{0:T(1024)} %param.17, f32[512]{0:T(512)S(1)} %add_rsqrt_fusion.1), kind=kOutput, calls=%fused_computation.16 | convolution fusion | flops 3224895488 | bytes 10491904 | tf_op jit(solution)/shard_map/dot_general | solution.py:53
  17.1 4.7 %copy.28 = bf16[512,3072]{0,1:T(8,128)(2,1)} copy(bf16[512,3072]{1,0:T(8,128)(2,1)} %convolution_convert_fusion) | data formatting | bytes 6291456 | tf_op jit(solution)/shard_map/convert_element_type | solution.py:53
  25.7 4.8 %all-to-all-start = ((bf16[4,512,3,256]{1,3,2,0:T(8,128)(2,1)}), bf16[4,512,3,256]{1,3,2,0:T(8,128)(2,1)}, u32[]{:S(2)}, u32[]{:S(2)}) async-start(bf16[4,512,3,256]{1,3,2,0:T(8,128)(2,1)} %pad_maximum_fusion), calls=%async_computation | async-start | bytes 6291456 | tf_op jit(solution)/shard_map/all_to_all | solution.py:56
  32.9 35.3 %all-to-all-done = bf16[4,512,3,256]{1,3,2,0:T(8,128)(2,1)} async-done(((bf16[4,512,3,256]{1,3,2,0:T(8,128)(2,1)}), bf16[4,512,3,256]{1,3,2,0:T(8,128)(2,1)}, u32[]{:S(2)}, u32[]{:S(2)}) %all-to-all-start) | async-done | bytes 3145760 | tf_op jit(solution)/shard_map/all_to_all | solution.py:56
  68.1 6.0 %copy.29 = bf16[4,512,3,256]{1,0,3,2:T(4,128)(2,1)} copy(bf16[4,512,3,256]{1,3,2,0:T(8,128)(2,1)} %all-to-all-done) | data formatting | bytes 6291456 | tf_op jit(solution)/shard_map/all_to_all | solution.py:56
  74.1 6.1 %reshape_reshape.4 = bf16[2048,3,4,64]{0,3,2,1:T(8,128)(2,1)} reshape(bf16[4,512,3,256]{1,0,3,2:T(4,128)(2,1)} %copy.29) | data formatting | bytes 6291456 | tf_op jit(solution)/shard_map/reshape;reshape | solution.py:60
  80.2 3.6 %slice_bitcast_fusion.4 = (bf16[2048,4,64]{0,2,1:T(8,128)(2,1)}, bf16[2048,4,64]{0,2,1:T(8,128)(2,1)S(1)}, bf16[2048,1,4,64]{0,3,2,1:T(8,128)(2,1)}) fusion(bf16[2048,3,4,64]{0,3,2,1:T(8,128)(2,1)} %reshape_reshape.4), kind=kLoop, calls=%fused_computation.34 | loop fusion | bytes 6291456 | tf_op jit(solution)/shard_map/squeeze | solution.py:62
  83.8 2.6 %reshape_squeeze.3 = bf16[4,512,4,64]{1,0,3,2:T(4,128)(2,1)} reshape(bf16[2048,1,4,64]{0,3,2,1:T(8,128)(2,1)} %get-tuple-element.80) | data formatting | bytes 2097152 | tf_op jit(solution)/shard_map/reshape;squeeze | solution.py:33
  88.9 3.8 %convolution_convert_fusion.1 = bf16[128,2048]{1,0:T(8,128)(2,1)} fusion(bf16[1024,2048]{1,0:T(8,128)(2,1)} %param.22, bf16[8,128,1024]{2,1,0:T(8,128)(2,1)} %all-gather.3.cloned.1.call-done, s32[]{:T(128)S(6)} %min.4, pred[]{:T(512)S(6)} %and.4), kind=kOutput, calls=%fused_computation.21 | convolution fusion | flops 537264128 | bytes 4980741 | tf_op jit(solution)/shard_map/dot_general | solution.py:72
  92.7 33.5 %while.2 = (s32[]{:T(128)}, bf16[4,512,4,64]{1,3,2,0:T(8,128)(2,1)}, bf16[4,512,4,64]{1,3,2,0:T(8,128)(2,1)}, bf16[2048,4,64]{0,2,1:T(8,128)(2,1)S(1)}, bf16[2048,4,64]{0,2,1:T(8,128)(2,1)}, /*index=5*/s32[]{:T(128)}) while((s32[]{:T(128)}, bf16[4,512,4,64]{1,3,2,0:T(8,128)(2,1)}, bf16[4,512,4,64]{1,3,2,0:T(8,128)(2,1)}, ...), condition=%wide.region_3.4_spmd, body=%wide.region_1.3_spmd.sunk | while | flops 1094842368 | bytes 40387680 | solution.py:33
  92.7 4.0 %fusion.49 = (f32[4,512]{1,0:T(4,128)S(1)}, f32[4,512,2048]{2,1,0:T(8,128)S(1)}) fusion(bf16[2048,4,64]{0,2,1:T(8,128)(2,1)S(1)} %get-tuple-element.139, bf16[4,512,4,64]{1,3,2,0:T(8,128)(2,1)} %get-tuple-element.138, s32[]{:T(128)} %get-tuple-element.130), kind=kOutput, calls=%fused_computation.2.clone.1 | convolution fusion | flops 545257472 | bytes 18096640 | tf_op jit(solution)/shard_map/while/body/eval_jaxpr/qhd,khd->hqk/dot_general | solution.py:24
  96.8 4.3 %fusion.50 = bf16[4,512,4,64]{1,3,2,0:T(8,128)(2,1)} fusion(bf16[4,512,4,64]{1,3,2,0:T(8,128)(2,1)} %get-tuple-element.131, s32[]{:T(128)} %get-tuple-element.130, bf16[2048,4,64]{0,2,1:T(8,128)(2,1)S(1)} %copy-done.4, f32[4,512,2048]{2,1,0:T(8,128)S(1)} %get-tuple-element.122, f32[4,512]{1,0:T(4,128)S(1)} %get-tuple-element.123), kind=kOutput, calls=%fused_computation.6.clone.1 | convolution fusion | flops 549584896 | bytes 18096640 | tf_op jit(solution)/shard_map/while/body/eval_jaxpr/hqk,khd->qhd/dot_general | solution.py:29
  101.1 4.1 %fusion.49 = (f32[4,512]{1,0:T(4,128)S(1)}, f32[4,512,2048]{2,1,0:T(8,128)S(1)}) fusion(bf16[2048,4,64]{0,2,1:T(8,128)(2,1)S(1)} %get-tuple-element.139, bf16[4,512,4,64]{1,3,2,0:T(8,128)(2,1)} %get-tuple-element.138, s32[]{:T(128)} %get-tuple-element.130), kind=kOutput, calls=%fused_computation.2.clone.1 | convolution fusion | flops 545257472 | bytes 18096640 | tf_op jit(solution)/shard_map/while/body/eval_jaxpr/qhd,khd->hqk/dot_general | solution.py:24
  105.2 4.3 %fusion.50 = bf16[4,512,4,64]{1,3,2,0:T(8,128)(2,1)} fusion(bf16[4,512,4,64]{1,3,2,0:T(8,128)(2,1)} %get-tuple-element.131, s32[]{:T(128)} %get-tuple-element.130, bf16[2048,4,64]{0,2,1:T(8,128)(2,1)S(1)} %copy-done.4, f32[4,512,2048]{2,1,0:T(8,128)S(1)} %get-tuple-element.122, f32[4,512]{1,0:T(4,128)S(1)} %get-tuple-element.123), kind=kOutput, calls=%fused_computation.6.clone.1 | convolution fusion | flops 549584896 | bytes 18096640 | tf_op jit(solution)/shard_map/while/body/eval_jaxpr/hqk,khd->qhd/dot_general | solution.py:29
  109.5 4.0 %fusion.49 = (f32[4,512]{1,0:T(4,128)S(1)}, f32[4,512,2048]{2,1,0:T(8,128)S(1)}) fusion(bf16[2048,4,64]{0,2,1:T(8,128)(2,1)S(1)} %get-tuple-element.139, bf16[4,512,4,64]{1,3,2,0:T(8,128)(2,1)} %get-tuple-element.138, s32[]{:T(128)} %get-tuple-element.130), kind=kOutput, calls=%fused_computation.2.clone.1 | convolution fusion | flops 545257472 | bytes 18096640 | tf_op jit(solution)/shard_map/while/body/eval_jaxpr/qhd,khd->hqk/dot_general | solution.py:24
  113.5 4.3 %fusion.50 = bf16[4,512,4,64]{1,3,2,0:T(8,128)(2,1)} fusion(bf16[4,512,4,64]{1,3,2,0:T(8,128)(2,1)} %get-tuple-element.131, s32[]{:T(128)} %get-tuple-element.130, bf16[2048,4,64]{0,2,1:T(8,128)(2,1)S(1)} %copy-done.4, f32[4,512,2048]{2,1,0:T(8,128)S(1)} %get-tuple-element.122, f32[4,512]{1,0:T(4,128)S(1)} %get-tuple-element.123), kind=kOutput, calls=%fused_computation.6.clone.1 | convolution fusion | flops 549584896 | bytes 18096640 | tf_op jit(solution)/shard_map/while/body/eval_jaxpr/hqk,khd->qhd/dot_general | solution.py:29
  117.8 4.0 %fusion.49 = (f32[4,512]{1,0:T(4,128)S(1)}, f32[4,512,2048]{2,1,0:T(8,128)S(1)}) fusion(bf16[2048,4,64]{0,2,1:T(8,128)(2,1)S(1)} %get-tuple-element.139, bf16[4,512,4,64]{1,3,2,0:T(8,128)(2,1)} %get-tuple-element.138, s32[]{:T(128)} %get-tuple-element.130), kind=kOutput, calls=%fused_computation.2.clone.1 | convolution fusion | flops 545257472 | bytes 18096640 | tf_op jit(solution)/shard_map/while/body/eval_jaxpr/qhd,khd->hqk/dot_general | solution.py:24
  121.9 4.3 %fusion.50 = bf16[4,512,4,64]{1,3,2,0:T(8,128)(2,1)} fusion(bf16[4,512,4,64]{1,3,2,0:T(8,128)(2,1)} %get-tuple-element.131, s32[]{:T(128)} %get-tuple-element.130, bf16[2048,4,64]{0,2,1:T(8,128)(2,1)S(1)} %copy-done.4, f32[4,512,2048]{2,1,0:T(8,128)S(1)} %get-tuple-element.122, f32[4,512]{1,0:T(4,128)S(1)} %get-tuple-element.123), kind=kOutput, calls=%fused_computation.6.clone.1 | convolution fusion | flops 549584896 | bytes 18096640 | tf_op jit(solution)/shard_map/while/body/eval_jaxpr/hqk,khd->qhd/dot_general | solution.py:29
  126.2 3.7 %all-to-all-start.1 = ((bf16[4,512,256]{1,2,0:T(8,128)(2,1)}), bf16[4,512,256]{1,2,0:T(8,128)(2,1)S(1)}, u32[]{:S(2)}, u32[]{:S(2)}) async-start(bf16[4,512,256]{1,2,0:T(8,128)(2,1)} %bitcast.12), calls=%async_computation.1 | async-start | bytes 2097152 | tf_op jit(solution)/shard_map/all_to_all | solution.py:63
  132.8 11.3 %all-to-all-done.1 = bf16[4,512,256]{1,2,0:T(8,128)(2,1)S(1)} async-done(((bf16[4,512,256]{1,2,0:T(8,128)(2,1)}), bf16[4,512,256]{1,2,0:T(8,128)(2,1)S(1)}, u32[]{:S(2)}, u32[]{:S(2)}) %all-to-all-start.1) | async-done | bytes 1048608 | tf_op jit(solution)/shard_map/all_to_all | solution.py:63
  144.1 2.7 %multiply_reduce_fusion = (f32[512]{0:T(512)S(1)}, f32[512,1024]{1,0:T(8,128)S(1)}) fusion(bf16[512,1024]{0,1:T(8,128)(2,1)S(1)} %bitcast.81, bf16[1024,1024]{1,0:T(8,128)(2,1)S(1)} %copy-done, bf16[1,512,1024]{2,1,0:T(8,128)(2,1)} %param.13), kind=kOutput, calls=%fused_computation.27 | convolution fusion | flops 1075838464 | bytes 6293504 | tf_op jit(solution)/shard_map/dot_general | solution.py:64
  152.0 3.9 %copy.31 = bf16[512,2048]{0,1:T(8,128)(2,1)} copy(bf16[512,2048]{1,0:T(8,128)(2,1)} %all-gather.5.cloned.1.call-done) | data formatting | bytes 4194304 | tf_op jit(solution)/shard_map/all_gather | solution.py:73
  156.0 5.5 %fusion.10 = (f32[16,512]{1,0:T(8,128)S(1)}, f32[16,512,512]{1,2,0:T(8,128)S(1)}) fusion(pred[512]{0:T(512)(128)(4,1)S(1)} %iota_compare_fusion, bf16[512,16,64]{0,2,1:T(8,128)(2,1)S(1)} %bitcast.84, bf16[512,2,16,64]{0,3,2,1:T(8,128)(2,1)} %bitcast.82), kind=kOutput, calls=%fused_computation.14 | convolution fusion | flops 549445632 | bytes 18907648 | tf_op jit(solution)/shard_map/while/body/eval_jaxpr/qhd,khd->hqk/dot_general | solution.py:24
  161.5 3.7 %fusion.15 = bf16[16,64,512]{2,1,0:T(8,128)(2,1)S(1)} fusion(f32[16,512,512]{1,2,0:T(8,128)S(1)} %get-tuple-element.88, f32[16,512]{1,0:T(8,128)S(1)} %get-tuple-element.87, pred[512]{0:T(512)(128)(4,1)S(1)} %iota_compare_fusion, bf16[512,2,16,64]{0,3,2,1:T(8,128)(2,1)S(1)} %bitcast.83), kind=kOutput, calls=%fused_computation.28 | convolution fusion | flops 554172416 | bytes 18907648 | tf_op jit(solution)/shard_map/while/body/eval_jaxpr/hqk,khd->qhd/dot_general | solution.py:29
  (45 shorter events, 17.9 us)
Async XLA Ops:
  6.5 137.6 %copy-start = (bf16[1024,1024]{1,0:T(8,128)(2,1)S(1)}, bf16[1024,1024]{1,0:T(8,128)(2,1)}, u32[]{:S(2)}) copy-start(bf16[1024,1024]{1,0:T(8,128)(2,1)} %param.19) | copy-start | bytes 6291460
  6.5 82.3 %all-gather.3.cloned.1.call-start = ((), (), s32[]{:S(2)}) async-start(), calls=%async_computation.2 | async-start | bytes 2359296 | tf_op jit(solution)/shard_map/all_gather | solution.py:71
  25.7 4.9 %copy-start.8 = (s32[8]{0:T(128)S(1)}, s32[8]{0:T(128)}, u32[]{:S(2)}) copy-start(s32[8]{0:T(128)} %param.16) | copy-start | bytes 100
  25.7 42.4 %all-to-all-start = ((bf16[4,512,3,256]{1,3,2,0:T(8,128)(2,1)}), bf16[4,512,3,256]{1,3,2,0:T(8,128)(2,1)}, u32[]{:S(2)}, u32[]{:S(2)}) async-start(bf16[4,512,3,256]{1,3,2,0:T(8,128)(2,1)} %pad_maximum_fusion), calls=%async_computation | async-start | bytes 6291456 | tf_op jit(solution)/shard_map/all_to_all | solution.py:56
  30.5 121.5 %all-gather.5.cloned.1.call-start = ((), (), s32[]{:S(2)}) async-start(), calls=%async_computation.3 | async-start | bytes 2621440 | tf_op jit(solution)/shard_map/all_gather | solution.py:73
  92.7 38.9 %copy-start.9 = (s32[8]{0:T(128)S(1)}, s32[8]{0:T(128)}, u32[]{:S(2)}) copy-start(s32[8]{0:T(128)} %param.15) | copy-start | bytes 100
  92.7 4.1 %copy-start.4 = (bf16[2048,4,64]{0,2,1:T(8,128)(2,1)S(1)}, bf16[2048,4,64]{0,2,1:T(8,128)(2,1)}, u32[]{:S(2)}) copy-start(bf16[2048,4,64]{0,2,1:T(8,128)(2,1)} %get-tuple-element.140) | copy-start | bytes 3145732 | tf_op jit(solution)/shard_map/while
  101.1 4.1 %copy-start.4 = (bf16[2048,4,64]{0,2,1:T(8,128)(2,1)S(1)}, bf16[2048,4,64]{0,2,1:T(8,128)(2,1)}, u32[]{:S(2)}) copy-start(bf16[2048,4,64]{0,2,1:T(8,128)(2,1)} %get-tuple-element.140) | copy-start | bytes 3145732 | tf_op jit(solution)/shard_map/while
  109.5 4.0 %copy-start.4 = (bf16[2048,4,64]{0,2,1:T(8,128)(2,1)S(1)}, bf16[2048,4,64]{0,2,1:T(8,128)(2,1)}, u32[]{:S(2)}) copy-start(bf16[2048,4,64]{0,2,1:T(8,128)(2,1)} %get-tuple-element.140) | copy-start | bytes 3145732 | tf_op jit(solution)/shard_map/while
  117.8 4.0 %copy-start.4 = (bf16[2048,4,64]{0,2,1:T(8,128)(2,1)S(1)}, bf16[2048,4,64]{0,2,1:T(8,128)(2,1)}, u32[]{:S(2)}) copy-start(bf16[2048,4,64]{0,2,1:T(8,128)(2,1)} %get-tuple-element.140) | copy-start | bytes 3145732 | tf_op jit(solution)/shard_map/while
  126.2 18.0 %all-to-all-start.1 = ((bf16[4,512,256]{1,2,0:T(8,128)(2,1)}), bf16[4,512,256]{1,2,0:T(8,128)(2,1)S(1)}, u32[]{:S(2)}, u32[]{:S(2)}) async-start(bf16[4,512,256]{1,2,0:T(8,128)(2,1)} %bitcast.12), calls=%async_computation.1 | async-start | bytes 2097152 | tf_op jit(solution)/shard_map/all_to_all | solution.py:63
  144.1 4.1 %copy-start.5 = (bf16[1024,1024]{1,0:T(8,128)(2,1)S(1)}, bf16[1024,1024]{1,0:T(8,128)(2,1)}, u32[]{:S(2)}) copy-start(bf16[1024,1024]{1,0:T(8,128)(2,1)} %param.21) | copy-start | bytes 6291460
  144.1 4.1 %copy-start.7 = (f32[1024]{0:T(1024)S(1)}, f32[1024]{0:T(1024)}, u32[]{:S(2)}) copy-start(f32[1024]{0:T(1024)} %param.20) | copy-start | bytes 12292
  146.9 1.3 copy-start.1
  156.0 5.5 %copy-start.3 = (bf16[512,2048]{0,1:T(8,128)(2,1)S(1)}, bf16[512,2048]{0,1:T(8,128)(2,1)}, u32[]{:S(2)}) copy-start(bf16[512,2048]{0,1:T(8,128)(2,1)} %copy.31) | copy-start | bytes 6291460
  161.5 3.8 %copy-start.2 = (f32[512,1024]{1,0:T(8,128)S(1)}, f32[512,1024]{1,0:T(8,128)}, u32[]{:S(2)}) copy-start(f32[512,1024]{1,0:T(8,128)} %copy-done.1) | copy-start | bytes 6291460
  161.5 3.8 %copy-start.6 = (bf16[1024,1024]{1,0:T(8,128)(2,1)S(1)}, bf16[1024,1024]{1,0:T(8,128)(2,1)}, u32[]{:S(2)}) copy-start(bf16[1024,1024]{1,0:T(8,128)(2,1)} %param.23) | copy-start | bytes 6291460
Sparse Core Ops, SparseCore 0:
  9.5 51.9 all-gather.2
  92.8 23.7 all-gather.4
